TPU v7x, 256 devices: a whole 4x4x8 slice. The times are simulated.
256 devices in a mesh: lon: 16 (over x_lo, z), lat: 16 (over y, x_hi, core).
Axes of the slice: x: 4 (x_hi: 2, x_lo: 2; x = x_hi * 2 + x_lo), y: 4, z: 8, core: 2. Of those that a mesh axis runs over, the one named last changes fastest.
Arguments:
- ensemble: bfloat16 [40, 2, 2048, 4096], P(None, None, 'lat', 'lon'), may hold values from -6 to 6
- gradient: bfloat16 [2, 2048, 4096], P(None, 'lat', 'lon'), may hold values from -6 to 6
Outputs:
- control: bfloat16 [40, 2, 2048, 4096], P(None, None, 'lat', 'lon')
All inputs are finite; a program needn't handle non-finite values.
Results may differ from a plain program's by a relative error of at most 0.0073.
Values may be sent and summed in bfloat16 or wider, within the bound.
A program may use at most 128 MiB of HBM per device.

v0:
```python
import jax
import jax.numpy as jnp
from jax import lax
from jax.sharding import PartitionSpec as P

HALF = 30


def padded(block, sides, width, periodic):
    for axis, dim in sides:
        count = lax.axis_size(axis)
        forward = [(i, i + 1) for i in range(count - 1)]
        if periodic:
            forward.append((count - 1, 0))
        backward = [(target, source) for source, target in forward]
        low = lax.ppermute(
            lax.slice_in_dim(block, block.shape[dim] - width, None, axis=dim), axis, forward
        )
        high = lax.ppermute(lax.slice_in_dim(block, 0, width, axis=dim), axis, backward)
        block = jnp.concatenate([low, block, high], axis=dim)
    return block


def kernel_matrix(block_len, half_width):
    spread = 1.0 * half_width
    row_index = jnp.arange(block_len + 2 * half_width)[:, None]
    col_index = jnp.arange(block_len)[None, :]
    offset = (row_index - col_index - half_width).astype(jnp.float32)
    offsets = jnp.arange(-half_width, half_width + 1).astype(jnp.float32)
    normalizer = jnp.sqrt(jnp.sum(jnp.exp(-offsets * offsets / (spread * spread))))
    weights = (
        jnp.where(
            jnp.abs(offset) <= half_width, jnp.exp(-offset * offset / (2.0 * spread * spread)), 0.0
        )
        / normalizer
    )
    return weights.astype(jnp.bfloat16)


def shards(ensemble, gradient):
    lat_rows = ensemble.shape[2]
    lon_width = ensemble.shape[3]
    product = (ensemble.astype(jnp.float32) * gradient.astype(jnp.float32)[None]).astype(
        jnp.bfloat16
    )
    lon_kernel = kernel_matrix(lon_width, HALF)
    lat_kernel = kernel_matrix(lat_rows, HALF)
    widened = padded(product, (("lon", 3),), HALF, True)
    lon_done = jnp.einsum(
        "mlap,pq->mlaq", widened, lon_kernel, preferred_element_type=jnp.float32
    ).astype(jnp.bfloat16)
    widened_lat = padded(lon_done, (("lat", 2),), HALF, False)
    return jnp.einsum(
        "mlpc,pq->mlqc", widened_lat, lat_kernel, preferred_element_type=jnp.float32
    ).astype(jnp.bfloat16)


def solution(mesh):
    placed = (P(None, None, "lat", "lon"), P(None, "lat", "lon"))
    return jax.shard_map(
        shards, mesh=mesh, in_specs=placed, out_specs=P(None, None, "lat", "lon"), check_vma=False
    )
```

profile of v0, /device:TPU:24, one launch (start us, length us, event | category | flops | bytes accessed | tf_op | source)
XLA Modules:
  0.0 85.8 jit_solution(6840097784120655996)
XLA Ops:
  0.0 1.0 %copy.6 = f32[2,128,256]{1,2,0:T(8,128)S(1)} copy(bf16[2,128,256]{2,1,0:T(8,128)(2,1)} %param.3) | data formatting | bytes 393216 | tf_op jit(solution)/shard_map/convert_element_type | solution.py:43
  1.0 7.9 %copy.5 = bf16[40,2,128,256]{2,3,1,0:T(8,128)(2,1)} copy(bf16[40,2,128,256]{3,2,1,0:T(8,128)(2,1)} %param.2) | data formatting | bytes 10485760 | tf_op args[0]
  8.9 4.0 %multiply_convert_fusion = bf16[40,2,128,256]{2,3,1,0:T(8,128)(2,1)S(1)} fusion(bf16[40,2,128,256]{2,3,1,0:T(8,128)(2,1)} %copy.5, f32[2,128,256]{1,2,0:T(8,128)S(1)} %copy.6), kind=kLoop, calls=%fused_computation | loop fusion | flops 7864320 | bytes 10747904 | tf_op jit(solution)/shard_map/convert_element_type | solution.py:43
  12.9 0.0 copy-start
  12.9 2.3 %copy-done = bf16[40,2,128,256]{2,3,1,0:T(8,128)(2,1)} copy-done((bf16[40,2,128,256]{2,3,1,0:T(8,128)(2,1)}, bf16[40,2,128,256]{2,3,1,0:T(8,128)(2,1)S(1)}, u32[]{:S(2)}) %copy-start) | copy-done | bytes 5242904
  15.3 0.4 fusion.55
  15.7 0.4 copy.8
  16.1 6.9 %collective-permute-start.1 = (bf16[40,2,128,30]{2,0,3,1:T(8,128)(2,1)S(1)}, bf16[40,2,128,30]{2,0,3,1:T(8,128)(2,1)S(1)}, u32[]{:S(2)}, u32[]{:S(2)}) collective-permute-start(bf16[40,2,128,30]{2,0,3,1:T(8,128)(2,1)S(1)} %copy.8), channel_id=1, source_target_pairs={{16,0},{32,16},{48,32},{64,48},{80,64},{96,80},{112,96},{128,112},... | collective-permute-start | bytes 1843208 | tf_op jit(solution)/shard_map/ppermute | solution.py:19
  22.9 0.4 copy.7
  23.3 0.1 collective-permute-start
  23.4 0.6 fusion.43
  24.7 11.3 %collective-permute-done.1 = bf16[40,2,128,30]{2,0,3,1:T(8,128)(2,1)S(1)} collective-permute-done((bf16[40,2,128,30]{2,0,3,1:T(8,128)(2,1)S(1)}, bf16[40,2,128,30]{2,0,3,1:T(8,128)(2,1)S(1)}, u32[]{:S(2)}, u32[]{:S(2)}) %collective-permute-start.1) | collective-permute-done | bytes 614432 | tf_op jit(solution)/shard_map/ppermute | solution.py:19
  36.0 0.2 copy.10
  36.2 4.6 %collective-permute-done = bf16[40,2,128,30]{2,0,3,1:T(8,128)(2,1)S(1)} collective-permute-done((bf16[40,2,128,30]{2,0,3,1:T(8,128)(2,1)S(1)}, bf16[40,2,128,30]{2,0,3,1:T(8,128)(2,1)S(1)}, u32[]{:S(2)}, u32[]{:S(2)}) %collective-permute-start) | collective-permute-done | bytes 614432 | tf_op jit(solution)/shard_map/ppermute | solution.py:16
  40.8 0.2 copy.9
  41.0 5.2 %fusion.12 = bf16[40,2,128,256]{3,2,1,0:T(8,128)(2,1)S(1)} fusion(bf16[40,2,128,30]{2,3,1,0:T(8,128)(2,1)S(1)} %copy.10, bf16[40,2,128,256]{2,3,1,0:T(8,128)(2,1)} %copy-done, bf16[40,2,128,30]{2,3,1,0:T(8,128)(2,1)S(1)} %copy.9, f32[]{:T(128)S(6)} %sqrt.4), kind=kOutput, calls=%fused_computation.14 | convolution fusion | flops 1679676416 | bytes 11714564 | tf_op jit(solution)/shard_map/mlap,pq->mlaq/dot_general | solution.py:49
  46.2 0.7 fusion.54
  46.9 0.7 copy.12
  47.6 3.1 %collective-permute-start.3 = (bf16[40,2,30,256]{3,0,2,1:T(8,128)(2,1)S(1)}, bf16[40,2,30,256]{3,0,2,1:T(8,128)(2,1)S(1)}, u32[]{:S(2)}, u32[]{:S(2)}) collective-permute-start(bf16[40,2,30,256]{3,0,2,1:T(8,128)(2,1)S(1)} %copy.12), channel_id=1, source_target_pairs={{1,0},{2,1},{3,2},{4,3},{5,4},{6,5},{7,6},{8,7},{9,8},{10,9},{11,1... | collective-permute-start | bytes 3686408 | tf_op jit(solution)/shard_map/ppermute | solution.py:19
  50.8 0.7 copy.11
  51.4 1.9 %collective-permute-start.2 = (bf16[40,2,30,256]{3,0,2,1:T(8,128)(2,1)S(1)}, bf16[40,2,30,256]{3,0,2,1:T(8,128)(2,1)S(1)}, u32[]{:S(2)}, u32[]{:S(2)}) collective-permute-start(bf16[40,2,30,256]{3,0,2,1:T(8,128)(2,1)S(1)} %copy.11), channel_id=1, source_target_pairs={{0,1},{1,2},{2,3},{3,4},{4,5},{5,6},{6,7},{7,8},{8,9},{9,10},{10,1... | collective-permute-start | bytes 3686408 | tf_op jit(solution)/shard_map/ppermute | solution.py:16
  53.4 21.2 %collective-permute-done.3 = bf16[40,2,30,256]{3,0,2,1:T(8,128)(2,1)S(1)} collective-permute-done((bf16[40,2,30,256]{3,0,2,1:T(8,128)(2,1)S(1)}, bf16[40,2,30,256]{3,0,2,1:T(8,128)(2,1)S(1)}, u32[]{:S(2)}, u32[]{:S(2)}) %collective-permute-start.3) | collective-permute-done | bytes 1228832 | tf_op jit(solution)/shard_map/ppermute | solution.py:19
  74.6 0.3 copy.14
  74.9 5.4 %collective-permute-done.2 = bf16[40,2,30,256]{3,0,2,1:T(8,128)(2,1)S(1)} collective-permute-done((bf16[40,2,30,256]{3,0,2,1:T(8,128)(2,1)S(1)}, bf16[40,2,30,256]{3,0,2,1:T(8,128)(2,1)S(1)}, u32[]{:S(2)}, u32[]{:S(2)}) %collective-permute-start.2) | collective-permute-done | bytes 1228832 | tf_op jit(solution)/shard_map/ppermute | solution.py:16
  80.3 0.3 copy.13
  80.6 5.1 %convert_bitcast_fusion = bf16[40,2,128,256]{3,2,1,0:T(8,128)(2,1)} fusion(bf16[40,2,30,256]{3,2,1,0:T(8,128)(2,1)S(1)} %copy.14, bf16[40,2,128,256]{3,2,1,0:T(8,128)(2,1)S(1)} %fusion.12, bf16[40,2,30,256]{3,2,1,0:T(8,128)(2,1)S(1)} %copy.13, f32[]{:T(128)S(6)} %sqrt.4), kind=kOutput, calls=%fused_computation.13 | convolution fusion | flops 1011649024 | bytes 12943364 | tf_op jit(solution)/shard_map/mlpc,pq->mlqc/dot_general | solution.py:53
Async XLA Ops:
  12.9 2.4 %copy-start = (bf16[40,2,128,256]{2,3,1,0:T(8,128)(2,1)}, bf16[40,2,128,256]{2,3,1,0:T(8,128)(2,1)S(1)}, u32[]{:S(2)}) copy-start(bf16[40,2,128,256]{2,3,1,0:T(8,128)(2,1)S(1)} %multiply_convert_fusion) | copy-start | bytes 15728644
  16.1 20.0 %collective-permute-start.1 = (bf16[40,2,128,30]{2,0,3,1:T(8,128)(2,1)S(1)}, bf16[40,2,128,30]{2,0,3,1:T(8,128)(2,1)S(1)}, u32[]{:S(2)}, u32[]{:S(2)}) collective-permute-start(bf16[40,2,128,30]{2,0,3,1:T(8,128)(2,1)S(1)} %copy.8), channel_id=1, source_target_pairs={{16,0},{32,16},{48,32},{64,48},{80,64},{96,80},{112,96},{128,112},... | collective-permute-start | bytes 1843208 | tf_op jit(solution)/shard_map/ppermute | solution.py:19
  23.3 17.5 %collective-permute-start = (bf16[40,2,128,30]{2,0,3,1:T(8,128)(2,1)S(1)}, bf16[40,2,128,30]{2,0,3,1:T(8,128)(2,1)S(1)}, u32[]{:S(2)}, u32[]{:S(2)}) collective-permute-start(bf16[40,2,128,30]{2,0,3,1:T(8,128)(2,1)S(1)} %copy.7), channel_id=1, source_target_pairs={{0,16},{16,32},{32,48},{48,64},{64,80},{80,96},{96,112},{112,128},... | collective-permute-start | bytes 1843208 | tf_op jit(solution)/shard_map/ppermute | solution.py:16
  47.6 27.0 %collective-permute-start.3 = (bf16[40,2,30,256]{3,0,2,1:T(8,128)(2,1)S(1)}, bf16[40,2,30,256]{3,0,2,1:T(8,128)(2,1)S(1)}, u32[]{:S(2)}, u32[]{:S(2)}) collective-permute-start(bf16[40,2,30,256]{3,0,2,1:T(8,128)(2,1)S(1)} %copy.12), channel_id=1, source_target_pairs={{1,0},{2,1},{3,2},{4,3},{5,4},{6,5},{7,6},{8,7},{9,8},{10,9},{11,1... | collective-permute-start | bytes 3686408 | tf_op jit(solution)/shard_map/ppermute | solution.py:19
  51.4 28.9 %collective-permute-start.2 = (bf16[40,2,30,256]{3,0,2,1:T(8,128)(2,1)S(1)}, bf16[40,2,30,256]{3,0,2,1:T(8,128)(2,1)S(1)}, u32[]{:S(2)}, u32[]{:S(2)}) collective-permute-start(bf16[40,2,30,256]{3,0,2,1:T(8,128)(2,1)S(1)} %copy.11), channel_id=1, source_target_pairs={{0,1},{1,2},{2,3},{3,4},{4,5},{5,6},{6,7},{7,8},{8,9},{9,10},{10,1... | collective-permute-start | bytes 3686408 | tf_op jit(solution)/shard_map/ppermute | solution.py:16
where the time goes:
time: 86.1 us; the launch traced here: 85.8 us
  waiting for transfers between devices  42.6 us (49%)
  local copies, waits for them, and re-layouts  15.4 us (18%)
  starting transfers between devices  12 us (14%)
  matrix products  10.4 us (12%)
  other arithmetic  4.6 us (5%)
    ppermute x2, waiting for transfers between devices, padded(): lax.ppermute(lax.slice_in_dim(block, 0, width, axis=dim), axis, backward)  32.5 us
    unnamed x3, local copies, waits for them, and re-layouts  10.3 us
    ppermute x2, waiting for transfers between devices, padded(): lax.ppermute(lax.slice_in_dim(block, block.shape[dim] - width, None, axis...  10 us
    ppermute x2, starting transfers between devices, padded(): lax.ppermute(lax.slice_in_dim(block, 0, width, axis=dim), axis, backward)  9.98 us
    dot_general x1, matrix products, shards(): jnp.einsum('mlap,pq->mlaq', widened, lon_kernel, preferred_element_type=j...  5.23 us
    dot_general x1, matrix products, shards(): jnp.einsum('mlpc,pq->mlqc', widened_lat, lat_kernel, preferred_element_ty...  5.14 us
    convert_element_type x1, other arithmetic, shards(): (ensemble.astype(jnp.float32) * gradient.astype(jnp.float32)[None]).astyp...  3.98 us
    slice x4, local copies, waits for them, and re-layouts, padded(): lax.slice_in_dim(block, block.shape[dim] - width, None, axis=dim)  2.15 us
  transfers between devices with their start and end apart: 4, of which 4 were waited for; matrix products, arithmetic and copies ran while one was open for 3% of the time, Pallas kernels for 0%

commit v1 on v0

v1 whole, which is shorter than its diff:
```python
import functools

import jax
import jax.numpy as jnp
import ml_dtypes
import numpy as np
from jax import lax
from jax.experimental import pallas as pl
from jax.experimental.pallas import tpu as pltpu
from jax.sharding import PartitionSpec as P

HALF = 30
GROUP = 8
SLOT = 32
WINDOW = 48
LON_AHEAD = 3
LAT_AHEAD = 3
MESH = pl.DeviceIdType.MESH
F32 = jnp.float32
BF16 = jnp.bfloat16


def kernel_values():
    offsets = np.arange(-HALF, HALF + 1, dtype=np.float64)
    normalizer = np.sqrt(np.sum(np.exp(-offsets * offsets / HALF**2)))
    values = np.exp(-offsets * offsets / (2.0 * HALF**2)) / normalizer
    return values.astype(np.float32).astype(ml_dtypes.bfloat16).astype(np.float32)


def banded(sources, targets):
    values = kernel_values()
    offset = sources - targets
    return np.where(np.abs(offset) <= HALF, values[np.clip(offset + HALF, 0, 2 * HALF)], 0.0)


def window_start(field, rows):
    return min(HALF * field // 16 * 16, rows - WINDOW)


def constants(lat_rows, lon_width):
    columns = np.arange(lon_width)
    lon = np.zeros((4, 2 * lon_width, lon_width), np.float32)
    for j in range(4):
        lon[j, :lon_width] = banded(columns[:, None], columns[None, :])
        first = lon_width + SLOT * j
        halo = np.arange(HALF)
        lon[j, first : first + HALF] = banded(halo[:, None] - HALF, columns[None, :])
        first += lon_width // 2
        lon[j, first : first + HALF] = banded(halo[:, None] + lon_width, columns[None, :])
    rows = np.arange(lat_rows)
    halo = np.arange(HALF)
    packed = GROUP * HALF
    lat = np.zeros((GROUP, lat_rows, lat_rows + 2 * WINDOW), np.float32)
    for j in range(GROUP):
        lat[j, :, :lat_rows] = banded(rows[None, :], rows[:, None])
        first = lat_rows + HALF * j - window_start(j, packed)
        lat[j, :, first : first + HALF] = banded(halo[None, :] - HALF, rows[:, None])
        first += WINDOW
        lat[j, :, first : first + HALF] = banded(halo[None, :] + lat_rows, rows[:, None])
    pick = np.zeros((2, packed, GROUP * 32), np.float32)
    for j in range(GROUP):
        for i in range(HALF):
            pick[0, HALF * j + i, 32 * j + i] = 1.0
            pick[1, HALF * j + i, 32 * j + 32 - HALF + i] = 1.0
    return [a.astype(ml_dtypes.bfloat16) for a in (lon, lat, pick)]


def body(
    n_lon, n_lat, chunks,
    ens_hbm, grad_hbm, lon_hbm, lat_hbm, pick_hbm,
    out_ref,
    ens, grad, lon_k, lat_k, pick, prod, done, lon_send, lon_halo, lat_send, lat_halo,
    const_sem, in_sem, lon_ssem, lon_rsem, lat_ssem, lat_rsem,
):
    lon_at = lax.axis_index("lon")
    lat_at = lax.axis_index("lat")
    lon_low = lax.rem(lon_at + n_lon - 1, n_lon)
    lon_high = lax.rem(lon_at + 1, n_lon)
    has_low = lat_at > 0
    has_high = lat_at < n_lat - 1
    lat_low = jnp.maximum(lat_at - 1, 0)
    lat_high = jnp.minimum(lat_at + 1, n_lat - 1)
    rows, width = prod.shape[1:]
    half = width // 2

    def chunk(c):
        return pl.ds(pl.multiple_of(c * GROUP, GROUP), GROUP)

    def load(c):
        return pltpu.make_async_copy(ens_hbm.at[chunk(c)], ens.at[chunk(c)], in_sem.at[c])

    pairs = ((grad_hbm, grad), (lon_hbm, lon_k), (lat_hbm, lat_k), (pick_hbm, pick))
    fixed = [pltpu.make_async_copy(s, d, const_sem.at[i]) for i, (s, d) in enumerate(pairs)]
    fixed[0].start()
    load(0).start()
    for copy in fixed[1:]:
        copy.start()
    for c in range(1, chunks):
        load(c).start()

    barrier = pltpu.get_barrier_semaphore()
    pl.semaphore_signal(barrier, inc=1, device_id={"lon": lon_low}, device_id_type=MESH)
    pl.semaphore_signal(barrier, inc=1, device_id={"lon": lon_high}, device_id_type=MESH)

    @pl.when(has_low)
    def _():
        pl.semaphore_signal(barrier, inc=1, device_id={"lat": lat_low}, device_id_type=MESH)

    @pl.when(has_high)
    def _():
        pl.semaphore_signal(barrier, inc=1, device_id={"lat": lat_high}, device_id_type=MESH)

    @pl.when(jnp.logical_not(has_low))
    def _():
        lat_halo[0] = jnp.zeros(lat_halo.shape[1:], BF16)

    @pl.when(jnp.logical_not(has_high))
    def _():
        lat_halo[1] = jnp.zeros(lat_halo.shape[1:], BF16)

    def lon_copy(side, c):
        return pltpu.make_async_remote_copy(
            src_ref=lon_send.at[side, c],
            dst_ref=lon_halo.at[side, c],
            send_sem=lon_ssem.at[side, c],
            recv_sem=lon_rsem.at[side, c],
            device_id={"lon": lon_high if side == 0 else lon_low},
            device_id_type=MESH,
        )

    def lat_copy(side, c):
        return pltpu.make_async_remote_copy(
            src_ref=lat_send.at[side, c],
            dst_ref=lat_halo.at[side, c],
            send_sem=lat_ssem.at[side, c],
            recv_sem=lat_rsem.at[side, c],
            device_id={"lat": lat_high if side == 0 else lat_low},
            device_id_type=MESH,
        )

    lane = lax.broadcasted_iota(jnp.int32, (rows, half), 1)

    def product(c):
        load(c).wait()
        for q in range(GROUP // 4):
            low = high = None
            for j in range(4):
                f = c * GROUP + 4 * q + j
                value = (ens[f].astype(F32) * grad[j % 2].astype(F32)).astype(BF16)
                prod[f] = value
                value = value.astype(F32)
                here_low = value[:, :half]
                here_high = pltpu.roll(value[:, half:], (SLOT * j + HALF) % half, 1)
                if j == 0:
                    low, high = here_low, here_high
                else:
                    here_low = pltpu.roll(here_low, SLOT * j, 1)
                    mine = lane >= SLOT * j
                    low = jnp.where(mine, here_low, low)
                    high = jnp.where(mine, here_high, high)
            lon_send[0, c, q] = high.astype(BF16)
            lon_send[1, c, q] = low.astype(BF16)

    def lon_start(c):
        lon_copy(0, c).start()
        lon_copy(1, c).start()

    def lon_sum(c):
        lon_copy(0, c).wait_recv()
        lon_copy(1, c).wait_recv()
        quads = GROUP // 4
        for j in range(4):
            left = [
                jnp.concatenate(
                    [prod[c * GROUP + 4 * q + j], lon_halo[0, c, q], lon_halo[1, c, q]], axis=1
                )
                for q in range(quads)
            ]
            total = jnp.dot(
                jnp.concatenate(left, axis=0), lon_k[j], preferred_element_type=F32
            ).astype(BF16)
            for q in range(quads):
                done[c * GROUP + 4 * q + j] = total[q * rows : (q + 1) * rows]
        first = [done[c * GROUP + j, :32] for j in range(GROUP)]
        last = [done[c * GROUP + j, rows - 32 :] for j in range(GROUP)]
        for side, edge in ((0, last), (1, first)):
            lat_send[side, c] = jnp.dot(
                pick[1 - side], jnp.concatenate(edge, axis=0), preferred_element_type=F32
            ).astype(BF16)

    def lat_start(c):
        @pl.when(has_high)
        def _():
            lat_copy(0, c).start()

        @pl.when(has_low)
        def _():
            lat_copy(1, c).start()

    def lat_sum(c):
        @pl.when(has_low)
        def _():
            lat_copy(0, c).wait_recv()

        @pl.when(has_high)
        def _():
            lat_copy(1, c).wait_recv()

        for j in range(GROUP):
            f = c * GROUP + j
            start = window_start(j, GROUP * HALF)
            right = jnp.concatenate(
                [done[f]] + [lat_halo[side, c, start : start + WINDOW] for side in range(2)],
                axis=0,
            )
            out_ref[f] = jnp.dot(lat_k[j], right, preferred_element_type=F32).astype(BF16)

    fixed[0].wait()
    product(0)
    peers = 2 + has_low.astype(jnp.int32) + has_high.astype(jnp.int32)
    pl.semaphore_wait(barrier, peers)
    lon_start(0)
    for copy in fixed[1:]:
        copy.wait()

    def step(t, carry):
        @pl.when(t < chunks)
        def _():
            product(t)
            lon_start(t)

        at_lon = t - LON_AHEAD

        @pl.when((at_lon >= 0) & (at_lon < chunks))
        def _():
            lon_sum(at_lon)
            lat_start(at_lon)

        at_lat = at_lon - LAT_AHEAD

        @pl.when(at_lat >= 0)
        def _():
            lat_sum(at_lat)

        return carry

    lax.fori_loop(1, chunks + LON_AHEAD + LAT_AHEAD, step, 0)

    def drain(c, carry):
        lon_copy(0, c).wait_send()
        lon_copy(1, c).wait_send()

        @pl.when(has_high)
        def _():
            lat_copy(0, c).wait_send()

        @pl.when(has_low)
        def _():
            lat_copy(1, c).wait_send()

        return carry

    lax.fori_loop(0, chunks, drain, 0)


def shards(n_lon, n_lat, ensemble, gradient):
    members, levels, rows, width = ensemble.shape
    fields = members * levels
    chunks = fields // GROUP
    lon, lat, pick = constants(rows, width)
    packed = GROUP * HALF
    quads = GROUP // 4
    any_space = pl.BlockSpec(memory_space=pl.ANY)
    out = pl.pallas_call(
        functools.partial(body, n_lon, n_lat, chunks),
        out_shape=jax.ShapeDtypeStruct((fields, rows, width), BF16),
        in_specs=[any_space] * 5,
        out_specs=pl.BlockSpec(memory_space=pltpu.VMEM),
        scratch_shapes=[
            pltpu.VMEM((fields, rows, width), BF16),
            pltpu.VMEM(gradient.shape, BF16),
            pltpu.VMEM(lon.shape, BF16),
            pltpu.VMEM(lat.shape, BF16),
            pltpu.VMEM(pick.shape, BF16),
            pltpu.VMEM((fields, rows, width), BF16),
            pltpu.VMEM((fields, rows, width), BF16),
            pltpu.VMEM((2, chunks, quads, rows, width // 2), BF16),
            pltpu.VMEM((2, chunks, quads, rows, width // 2), BF16),
            pltpu.VMEM((2, chunks, packed, width), BF16),
            pltpu.VMEM((2, chunks, packed, width), BF16),
            pltpu.SemaphoreType.DMA((4,)),
            pltpu.SemaphoreType.DMA((chunks,)),
            pltpu.SemaphoreType.DMA((2, chunks)),
            pltpu.SemaphoreType.DMA((2, chunks)),
            pltpu.SemaphoreType.DMA((2, chunks)),
            pltpu.SemaphoreType.DMA((2, chunks)),
        ],
        compiler_params=pltpu.CompilerParams(
            collective_id=0, has_side_effects=True, vmem_limit_bytes=56 * 1024 * 1024
        ),
    )(ensemble.reshape(fields, rows, width), gradient, lon, lat, pick)
    return out.reshape(ensemble.shape)


def solution(mesh):
    placed = (P(None, None, "lat", "lon"), P(None, "lat", "lon"))
    return jax.shard_map(
        functools.partial(shards, mesh.shape["lon"], mesh.shape["lat"]),
        mesh=mesh,
        in_specs=placed,
        out_specs=P(None, None, "lat", "lon"),
        check_vma=False,
    )
```

time: 86.1 us -> 61.6 us (0.72)
  Pallas kernels: 0 us -> 55.3 us
  waiting for transfers between devices: 42.6 us -> 0 us
  starting transfers between devices: 12 us -> 0 us
  matrix products: 10.4 us -> 0 us
  local copies, waits for them, and re-layouts: 15.4 us -> 5.49 us
  other arithmetic: 4.6 us -> 0 us
    pallas_call x0 -> x1, Pallas kernels: none -> 55.3 us  [shards(): pl.pallas_call(functools.partial(body, n_lon, n_lat, chunks), out_shape=j...]
    ppermute x4 -> x0, waiting for transfers between devices: 42.6 us -> none  [the longest x2 32.5 us: padded(): lax.ppermute(lax.slice_in_dim(block, 0, width, axis=dim), axis, backward)]
    ppermute x4 -> x0, starting transfers between devices: 12 us -> none  [the longest x2 9.98 us: padded(): lax.ppermute(lax.slice_in_dim(block, 0, width, axis=dim), axis, backward)]
    dot_general x2 -> x0, matrix products: 10.4 us -> none  [the longest x1 5.23 us: shards(): jnp.einsum('mlap,pq->mlaq', widened, lon_kernel, preferred_element_type=j...]
    unnamed x3 -> x1, local copies, waits for them, and re-layouts: 10.3 us -> 5.49 us
    convert_element_type x1 -> x0, other arithmetic: 3.98 us -> none  [shards(): (ensemble.astype(jnp.float32) * gradient.astype(jnp.float32)[None]).astyp...]
    slice x6 -> x0, local copies, waits for them, and re-layouts: 3.25 us -> none  [the longest x4 2.15 us: padded(): lax.slice_in_dim(block, block.shape[dim] - width, None, axis=dim)]
    convert_element_type x1 -> x0, local copies, waits for them, and re-layouts: 1 us -> none  [shards(): gradient.astype(jnp.float32)[None]]
  transfers between devices with their start and end apart: 4 -> 0, of which waited for: 4 -> 0; matrix products, arithmetic and copies ran while one was open for 3% -> 0% of each run, Pallas kernels for 0% -> 0%
where the time goes in v1:
time: 61.6 us; the launch traced here: 60.7 us
  Pallas kernels  55.3 us (90%)
  local copies, waits for them, and re-layouts  5.49 us (9%)
    pallas_call x1, Pallas kernels, shards(): pl.pallas_call(functools.partial(body, n_lon, n_lat, chunks), out_shape=j...  55.3 us
    unnamed x1, local copies, waits for them, and re-layouts  5.49 us

profile of v1, /device:TPU:24, one launch (start us, length us, event | category | flops | bytes accessed | tf_op | source)
XLA Modules:
  0.0 60.7 jit_solution(13857103124122832553)
XLA Ops:
  0.0 55.3 %shard_map.55 = bf16[80,128,256]{2,1,0:T(8,128)(2,1)} custom-call(bf16[80,128,256]{2,1,0:T(8,128)(2,1)} %bitcast.3, bf16[2,128,256]{2,1,0:T(8,128)(2,1)} %grad_hbm.1, bf16[4,512,256]{2,1,0:T(8,128)(2,1)} %constant.6.clone.lon_hbm, bf16[8,128,224]{2,1,0:T(8,128)(2,1)} %constant.7.clone.lat_hbm, bf16[2,240,256]{2,1,0:T(8,128)(2,1)} %constant.8.clone.pick_hbm), custom_call_target="tpu_custom_call" | custom-call | tf_op jit(solution)/shard_map/pallas_call | solution.py:274
  55.3 5.5 %copy.7 = bf16[40,2,128,256]{3,2,1,0:T(8,128)(2,1)} copy(bf16[40,2,128,256]{3,2,1,0:T(8,128)(2,1)} %bitcast.2) | data formatting | bytes 10485760

commit v2 on v1

--- a/solution.py
+++ b/solution.py
@@ -13,8 +13,12 @@
 GROUP = 8
 SLOT = 32
 WINDOW = 48
-LON_AHEAD = 3
-LAT_AHEAD = 3
+LON_AHEAD = 6
+LAT_AHEAD = 4
+DIRECT = 3
+ROUTES = 3
+RELAY_AFTER = 4
+LAG = 3
 MESH = pl.DeviceIdType.MESH
 F32 = jnp.float32
 BF16 = jnp.bfloat16
@@ -70,7 +74,7 @@
     ens_hbm, grad_hbm, lon_hbm, lat_hbm, pick_hbm,
     out_ref,
     ens, grad, lon_k, lat_k, pick, prod, done, lon_send, lon_halo, lat_send, lat_halo,
-    const_sem, in_sem, lon_ssem, lon_rsem, lat_ssem, lat_rsem,
+    relay_box, near_sem, twin_sem, const_sem, in_sem, relay_ssem, relay_rsem, lon_ssem, lon_rsem, lat_ssem, lat_rsem,
 ):
     lon_at = lax.axis_index("lon")
     lat_at = lax.axis_index("lat")
@@ -80,6 +84,17 @@
     has_high = lat_at < n_lat - 1
     lat_low = jnp.maximum(lat_at - 1, 0)
     lat_high = jnp.minimum(lat_at + 1, n_lat - 1)
+    row = n_lon // 2
+    place = lax.rem(lon_at, row)
+    mine = lon_at - place
+    other = row - mine
+    upper = place >= row // 2
+    relay_side = jnp.where(upper, 0, 1)
+    depth = jnp.where(upper, row - 1 - place, place)
+    relays = (depth > 0) & (depth <= ROUTES)
+    twin = other + place
+    toward = mine + jnp.where(upper, jnp.minimum(place + 1, row - 1), jnp.maximum(place - 1, 0))
+    relay_to = mine + jnp.where(upper, 0, row - 1)
     rows, width = prod.shape[1:]
     half = width // 2
 
@@ -102,6 +117,10 @@
     pl.semaphore_signal(barrier, inc=1, device_id={"lon": lon_low}, device_id_type=MESH)
     pl.semaphore_signal(barrier, inc=1, device_id={"lon": lon_high}, device_id_type=MESH)
 
+    @pl.when(depth == 0)
+    def _():
+        pl.semaphore_signal(barrier, inc=1, device_id={"lon": twin}, device_id_type=MESH)
+
     @pl.when(has_low)
     def _():
         pl.semaphore_signal(barrier, inc=1, device_id={"lat": lat_low}, device_id_type=MESH)
@@ -125,6 +144,30 @@
             send_sem=lon_ssem.at[side, c],
             recv_sem=lon_rsem.at[side, c],
             device_id={"lon": lon_high if side == 0 else lon_low},
+            device_id_type=MESH,
+        )
+
+    def slot(c):
+        return jnp.maximum(c - DIRECT, 0) // ROUTES
+
+    def seam_copy(side, c):
+        route = 1 + lax.rem(jnp.maximum(c - DIRECT, 0), ROUTES)
+        return pltpu.make_async_remote_copy(
+            src_ref=lon_send.at[side, c],
+            dst_ref=relay_box.at[slot(c)],
+            send_sem=lon_ssem.at[side, c],
+            recv_sem=relay_rsem.at[slot(c)],
+            device_id={"lon": other + (row - 1 - route if side == 0 else route)},
+            device_id_type=MESH,
+        )
+
+    def relay_copy(c):
+        return pltpu.make_async_remote_copy(
+            src_ref=relay_box.at[slot(c)],
+            dst_ref=lon_halo.at[relay_side, c],
+            send_sem=relay_ssem.at[slot(c)],
+            recv_sem=lon_rsem.at[relay_side, c],
+            device_id={"lon": relay_to},
             device_id_type=MESH,
         )
 
@@ -161,9 +204,25 @@
             lon_send[0, c, q] = high.astype(BF16)
             lon_send[1, c, q] = low.astype(BF16)
 
+    def seam_start(c):
+        for side, end in ((0, row - 1), (1, 0)):
+
+            @pl.when(place == end)
+            def _():
+                seam_copy(side, c).start()
+
     def lon_start(c):
-        lon_copy(0, c).start()
-        lon_copy(1, c).start()
+        for side, end in ((0, row - 1), (1, 0)):
+
+            @pl.when((place != end) | (c < DIRECT))
+            def _():
+                lon_copy(side, c).start()
+
+    def relay(c):
+        @pl.when(relays & (c >= DIRECT) & (1 + lax.rem(jnp.maximum(c - DIRECT, 0), ROUTES) == depth))
+        def _():
+            seam_copy(0, c).wait_recv()
+            relay_copy(c).start()
 
     def lon_sum(c):
         lon_copy(0, c).wait_recv()
@@ -218,16 +277,55 @@
     fixed[0].wait()
     product(0)
     peers = 2 + has_low.astype(jnp.int32) + has_high.astype(jnp.int32)
+    peers += jnp.where(depth == 0, 1, 0)
     pl.semaphore_wait(barrier, peers)
     lon_start(0)
     for copy in fixed[1:]:
         copy.wait()
 
+    @pl.when(depth == ROUTES - 1)
+    def _():
+        pl.semaphore_signal(near_sem, inc=1, device_id={"lon": toward}, device_id_type=MESH)
+
+    def announce():
+        @pl.when(depth < ROUTES - 1)
+        def _():
+            pl.semaphore_wait(near_sem, 1)
+
+        @pl.when((depth > 0) & (depth < ROUTES - 1))
+        def _():
+            pl.semaphore_signal(near_sem, inc=1, device_id={"lon": toward}, device_id_type=MESH)
+
+        @pl.when(depth == 0)
+        def _():
+            pl.semaphore_signal(twin_sem, inc=1, device_id={"lon": twin}, device_id_type=MESH)
+
     def step(t, carry):
+        @pl.when(t == 2)
+        def _():
+            announce()
+
+        @pl.when((t == DIRECT) & (depth == 0))
+        def _():
+            pl.semaphore_wait(twin_sem, 1)
+
         @pl.when(t < chunks)
         def _():
             product(t)
-            lon_start(t)
+
+            @pl.when(t >= DIRECT)
+            def _():
+                seam_start(t)
+
+            @pl.when(t < DIRECT)
+            def _():
+                lon_start(t)
+
+        at_send = t - LAG
+
+        @pl.when((at_send >= DIRECT) & (at_send < chunks))
+        def _():
+            lon_start(at_send)
 
         at_lon = t - LON_AHEAD
 
@@ -236,6 +334,12 @@
             lon_sum(at_lon)
             lat_start(at_lon)
 
+        at_relay = t - RELAY_AFTER
+
+        @pl.when((at_relay >= DIRECT) & (at_relay < chunks))
+        def _():
+            relay(at_relay)
+
         at_lat = at_lon - LAT_AHEAD
 
         @pl.when(at_lat >= 0)
@@ -247,6 +351,10 @@
     lax.fori_loop(1, chunks + LON_AHEAD + LAT_AHEAD, step, 0)
 
     def drain(c, carry):
+        @pl.when(relays & (c >= DIRECT) & (1 + lax.rem(jnp.maximum(c - DIRECT, 0), ROUTES) == depth))
+        def _():
+            relay_copy(c).wait_send()
+
         lon_copy(0, c).wait_send()
         lon_copy(1, c).wait_send()
 
@@ -261,6 +369,17 @@
         return carry
 
     lax.fori_loop(0, chunks, drain, 0)
+
+
+def store(chunks, from_ref, to_ref, sem):
+    copies = []
+    for c in range(chunks):
+        part = pl.ds(c * GROUP, GROUP)
+        copies.append(pltpu.make_async_copy(from_ref.at[part], to_ref.at[part], sem.at[c]))
+    for copy in copies:
+        copy.start()
+    for copy in copies:
+        copy.wait()
 
 
 def shards(n_lon, n_lat, ensemble, gradient):
@@ -270,11 +389,11 @@
     lon, lat, pick = constants(rows, width)
     packed = GROUP * HALF
     quads = GROUP // 4
-    any_space = pl.BlockSpec(memory_space=pl.ANY)
+    in_hbm = pl.BlockSpec(memory_space=pltpu.HBM)
     out = pl.pallas_call(
         functools.partial(body, n_lon, n_lat, chunks),
-        out_shape=jax.ShapeDtypeStruct((fields, rows, width), BF16),
-        in_specs=[any_space] * 5,
+        out_shape=pltpu.VMEM((fields, rows, width), BF16),
+        in_specs=[in_hbm] * 5,
         out_specs=pl.BlockSpec(memory_space=pltpu.VMEM),
         scratch_shapes=[
             pltpu.VMEM((fields, rows, width), BF16),
@@ -288,17 +407,30 @@
             pltpu.VMEM((2, chunks, quads, rows, width // 2), BF16),
             pltpu.VMEM((2, chunks, packed, width), BF16),
             pltpu.VMEM((2, chunks, packed, width), BF16),
+            pltpu.VMEM((pl.cdiv(chunks - DIRECT, ROUTES), quads, rows, width // 2), BF16),
+            pltpu.SemaphoreType.REGULAR,
+            pltpu.SemaphoreType.REGULAR,
             pltpu.SemaphoreType.DMA((4,)),
             pltpu.SemaphoreType.DMA((chunks,)),
+            pltpu.SemaphoreType.DMA((pl.cdiv(chunks - DIRECT, ROUTES),)),
+            pltpu.SemaphoreType.DMA((pl.cdiv(chunks - DIRECT, ROUTES),)),
             pltpu.SemaphoreType.DMA((2, chunks)),
             pltpu.SemaphoreType.DMA((2, chunks)),
             pltpu.SemaphoreType.DMA((2, chunks)),
             pltpu.SemaphoreType.DMA((2, chunks)),
         ],
         compiler_params=pltpu.CompilerParams(
-            collective_id=0, has_side_effects=True, vmem_limit_bytes=56 * 1024 * 1024
+            collective_id=0, has_side_effects=True, vmem_limit_bytes=61_700_000
         ),
     )(ensemble.reshape(fields, rows, width), gradient, lon, lat, pick)
+    out = pl.pallas_call(
+        functools.partial(store, chunks),
+        out_shape=jax.ShapeDtypeStruct((fields, rows, width), BF16),
+        in_specs=[pl.BlockSpec(memory_space=pltpu.VMEM)],
+        out_specs=in_hbm,
+        scratch_shapes=[pltpu.SemaphoreType.DMA((chunks,))],
+        compiler_params=pltpu.CompilerParams(vmem_limit_bytes=12 * 1024 * 1024),
+    )(pltpu.with_memory_space_constraint(out, pltpu.VMEM))
     return out.reshape(ensemble.shape)
 
 

time: 61.6 us -> 47 us (0.76)
  the two profiles are of different devices: /device:TPU:24 before, /device:TPU:33 now
where the time goes in v2:
time: 47 us; the launch traced here: 46.9 us
  Pallas kernels  46.9 us (100%)
    pallas_call x1, Pallas kernels, shards(): pl.pallas_call(functools.partial(body, n_lon, n_lat, chunks), out_shape=p...  44.5 us
    pallas_call x1, Pallas kernels, shards(): pl.pallas_call(functools.partial(store, chunks), out_shape=jax.ShapeDtype...  2.42 us

profile of v2, /device:TPU:33, one launch (start us, length us, event | category | flops | bytes accessed | tf_op | source)
XLA Modules:
  0.0 46.9 jit_solution(9794578897313675847)
XLA Ops:
  0.0 44.5 %shard_map.55.from_ref = bf16[80,128,256]{2,1,0:T(8,128)(2,1)S(1)} custom-call(bf16[80,128,256]{2,1,0:T(8,128)(2,1)} %bitcast.2, bf16[2,128,256]{2,1,0:T(8,128)(2,1)} %grad_hbm.1, bf16[4,512,256]{2,1,0:T(8,128)(2,1)} %constant.6.clone.lon_hbm, bf16[8,128,224]{2,1,0:T(8,128)(2,1)} %constant.7.clone.lat_hbm, bf16[2,240,256]{2,1,0:T(8,128)(2,1)} %constant.8.clone.pick_hbm), custom_call_target="tpu_custom_call" | custom-call | tf_op jit(solution)/shard_map/pallas_call | solution.py:393
  44.5 2.4 %shard_map.56 = bf16[80,128,256]{2,1,0:T(8,128)(2,1)} custom-call(bf16[80,128,256]{2,1,0:T(8,128)(2,1)S(1)} %shard_map.55.from_ref), custom_call_target="tpu_custom_call" | custom-call | tf_op jit(solution)/shard_map/pallas_call | solution.py:426
